TPU v7x, 768 devices: a whole 4x8x12 slice. The times are simulated.
768 devices in a mesh: row: 192 (over z, y, core), col: 4 (over x).
Axes of the slice: x: 4, y: 8, z: 12, core: 2. Of those that a mesh axis runs over, the one named last changes fastest.
Arguments:
- fine_matrix: bfloat16 [49152, 1536], P('row', 'col'), may hold values from -0.75 to 0.75
- fine_columns: int32 [768, 24], P('row'), may hold values from 0 to 767, as said below
- fine_counts: int32 [768], P('row'), may hold values from 12 to 24, as said below
- prolong: bfloat16 [49152, 128], P('row'), may hold values from -6 to 6
- prolong_columns: int32 [768, 2], P('row'), may hold values from 0 to 383
- restrict_rows: bfloat16 [24576, 256], P('row'), may hold values from -0.375 to 0.375
- coarse_pattern: int32 [192, 48], P('row'), may hold values from -1 to 383, as said below
Outputs:
- coarse_operator: float32 [24576, 3072], P('row', 'col')
Inputs may be any that keep to these rules, and one draw needn't show every extreme that they name: Only the first fine_counts[i] block slots of fine brick i are live. `fine_columns`: at most 4 block slots of each fine brick couple to a brick more than 8 bricks away, counting cyclically over the 768 bricks. `coarse_pattern`: each row holds distinct coarse brick numbers and -1 in slots left empty; every coarse brick reached by a live product of the slab is listed.
All inputs are finite; a program needn't handle non-finite values.
Results may differ from a plain program's by a relative error of at most 0.00035.
Values may be sent and summed in bfloat16 or wider, within the bound.
A program may use at most 32 MiB of HBM per device.

v0:
```python
import jax
import jax.numpy as jnp
from jax import lax
from jax.sharding import PartitionSpec as P

BRICK = 64
P_SLOTS = 2


def make_folder(targets, totals, pieces):
    piece_blocks, piece_columns = pieces
    arrived = piece_columns.shape[0]
    matches = targets[:, None] == jnp.arange(arrived, dtype=jnp.int32)[None, :]
    gathered = jnp.einsum(
        "mn,nbc->mbc",
        matches.astype(jnp.bfloat16),
        piece_blocks,
        preferred_element_type=jnp.float32,
    )
    picked = totals[1] + jnp.sum(
        jnp.where(matches[:, :, None], piece_columns[None, :, :], 0), axis=1
    )
    return (gathered, picked)


def local(
    fine_matrix, fine_columns, fine_counts, prolong, prolong_columns, restrict_rows, coarse_pattern
):
    bricks = fine_counts.shape[0]
    share_width = fine_matrix.shape[1] // BRICK
    col_index = lax.axis_index("col")
    owned_first = col_index * share_width
    live_slots = (owned_first + jnp.arange(share_width, dtype=jnp.int32))[None, :] < fine_counts[
        :, None
    ]
    blocks = prolong.reshape(bricks, BRICK, P_SLOTS * BRICK)
    targets = lax.dynamic_slice_in_dim(fine_columns, owned_first, share_width, 1).reshape(-1)
    empty_sel = (
        jnp.zeros((targets.shape[0], BRICK, P_SLOTS * BRICK), jnp.float32),
        jnp.zeros((targets.shape[0], P_SLOTS), jnp.int32),
    )
    chosen, reached = make_folder(
        targets,
        empty_sel,
        (
            lax.all_gather(blocks, "row", axis=0, tiled=True),
            lax.all_gather(prolong_columns, "row", axis=0, tiled=True),
        ),
    )
    chosen = chosen.astype(jnp.bfloat16).reshape(bricks, share_width, BRICK, P_SLOTS * BRICK)
    reached = reached.reshape(bricks, share_width, P_SLOTS)
    a_blocks = fine_matrix.reshape(bricks, BRICK, share_width, BRICK)
    products = jnp.einsum("iakb,ikbc->ikac", a_blocks, chosen, preferred_element_type=jnp.float32)
    products = products.reshape(bricks, share_width, BRICK, P_SLOTS, BRICK)
    pattern = coarse_pattern[0]
    matches = (
        (reached[:, :, :, None] == pattern[None, None, None, :]) & live_slots[:, :, None, None]
    ).astype(jnp.float32)
    partial_value = jnp.einsum(
        "ikqs,ikaqc->iasc", matches, products, precision=lax.Precision.HIGHEST
    )
    partial_value = partial_value.reshape(bricks * BRICK, pattern.shape[0] * BRICK)
    restrict = restrict_rows.astype(jnp.float32)
    owned_sums = lax.psum_scatter(partial_value, "col", scatter_dimension=1, tiled=True)
    return jnp.dot(restrict, owned_sums, precision=lax.Precision.HIGHEST)


def solution(mesh):
    return jax.shard_map(
        local,
        mesh=mesh,
        in_specs=(
            P("row", "col"),
            P("row", None),
            P("row"),
            P("row", None),
            P("row", None),
            P("row", None),
            P("row", None),
        ),
        out_specs=P("row", "col"),
        check_vma=False,
    )
```

profile of v0, /device:TPU:1, one launch (start us, length us, event | category | flops | bytes accessed | tf_op | source)
XLA Modules:
  0.0 225.4 jit_solution(13649942291521526214)
XLA Ops:
  6.5 0.0 copy-start
  6.5 0.0 all-gather.3.cloned.1.call-start
  6.5 0.7 all-gather.3.cloned.1.call-update
  7.3 0.0 reduce-scatter.2.cloned.1.call-start
  7.3 0.8 constant_dynamic-slice_fusion
  8.1 0.1 eq.36
  8.2 81.6 %all-gather = s32[192,4,2]{1,2,0:T(2,128)S(1)} all-gather(s32[1,4,2]{1,2,0:T(2,128)} %bitcast.34), channel_id=1, replica_groups=mesh['row'=192,'col'=4] {'row'}, dimensions={0}, use_global_device_ids=true | all-gather | bytes 6176 | tf_op jit(solution)/shard_map/all_gather | solution.py:47
  89.7 0.1 reshape.80
  89.9 0.1 iota_compare_fusion
  90.0 0.1 select_reduce_fusion
  90.1 0.1 eq.40
  90.2 1.2 reshape.84
  91.5 0.7 broadcast_compare_fusion
  92.2 0.0 copy-start.1
  92.2 57.7 %all-gather.3.cloned.1.call-done = bf16[768,64,128]{2,1,0:T(8,128)(2,1)} async-done(((bf16[4,64,128]{2,1,0:T(8,128)(2,1)}), bf16[768,64,128]{2,1,0:T(8,128)(2,1)}) %all-gather.3.cloned.1.call-update) | async-done | bytes 12582928 | tf_op jit(solution)/shard_map/all_gather | solution.py:46
  149.9 11.2 %fusion.3 = bf16[24,64,128]{2,0,1:T(8,128)(2,1)S(1)} fusion(bf16[768,64,128]{2,1,0:T(8,128)(2,1)} %all-gather.3.cloned.1.call-done, s32[24]{0:T(128)S(1)} %eq.36), kind=kOutput, calls=%fused_computation.5 | convolution fusion | flops 302204928 | bytes 12976224 | tf_op jit(solution)/shard_map/mn,nbc->mbc/dot_general | solution.py:14
  161.1 0.1 copy.32
  161.2 0.3 convolution_bitcast_fusion.1
  161.5 0.9 reshape.77
  162.4 0.0 copy-done.1
  162.4 5.4 %convolution_bitcast_fusion = f32[4,64,48,64]{3,2,1,0:T(8,128)} fusion(f32[4,6,64,2,64]{4,3,2,1,0:T(2,128)S(1)} %reshape.77, s32[48]{0:T(128)S(1)} %bitcast.35, s32[4,6,2]{1,2,0:T(2,128)S(1)} %copy.36, pred[4,6]{1,0:T(4,128)(4,1)S(1)} %broadcast_compare_fusion), kind=kOutput, calls=%fused_computation.2 | convolution fusion | flops 113250816 | bytes 3932568 | tf_op jit(solution)/shard_map/ikqs,ikaqc->iasc/dot_general | solution.py:59
  167.8 5.8 %reshape.78 = f32[256,3072]{1,0:T(8,128)} reshape(f32[4,64,48,64]{3,2,1,0:T(8,128)} %convolution_bitcast_fusion) | data formatting | bytes 6291456 | tf_op jit(solution)/shard_map/reshape | solution.py:62
  173.6 0.0 reduce-scatter.2.cloned.1.call-update
  173.6 42.0 %reduce-scatter.2.cloned.1.call-done = f32[256,768]{1,0:T(8,128)} async-done(((f32[256,3072]{1,0:T(8,128)}), f32[256,768]{1,0:T(8,128)}) %reduce-scatter.2.cloned.1.call-update) | async-done | bytes 786448 | tf_op jit(solution)/shard_map/reduce_scatter | solution.py:64
  215.7 0.0 copy-done
  215.7 1.9 convolution_bitcast_fusion.2
  217.6 0.9 copy.38
  (3 shorter events, 0.0 us)
Async XLA Ops:
  6.5 209.1 %copy-start = (bf16[128,256]{1,0:T(8,128)(2,1)S(1)}, bf16[128,256]{1,0:T(8,128)(2,1)}, u32[]{:S(2)}) copy-start(bf16[128,256]{1,0:T(8,128)(2,1)} %param.12) | copy-start | bytes 196612
  6.5 143.3 %all-gather.3.cloned.1.call-start = ((), (), s32[]{:S(2)}) async-start(), calls=%async_computation.1 | async-start | bytes 12648448 | tf_op jit(solution)/shard_map/all_gather | solution.py:46
  7.3 208.4 %reduce-scatter.2.cloned.1.call-start = ((), (), s32[]{:S(2)}) async-start(), calls=%async_computation.2 | async-start | bytes 3932160 | tf_op jit(solution)/shard_map/reduce_scatter | solution.py:64
  92.2 70.2 %copy-start.1 = (s32[1,48]{1,0:T(1,128)S(1)}, s32[1,48]{1,0:T(1,128)}, u32[]{:S(2)}) copy-start(s32[1,48]{1,0:T(1,128)} %param.13) | copy-start | bytes 580
Sparse Core Ops, SparseCore 0:
  11.1 138.7 all-gather.2
  173.7 41.8 reduce-scatter.1
where the time goes:
time: 226 us; the launch traced here: 225 us
  waiting for transfers between devices  100 us (44%)
  blocking collectives  81.6 us (36%)
  matrix products  18.9 us (8%)
  between operations  13.5 us (6%)
  local copies, waits for them, and re-layouts  10 us (4%)
    all_gather x1, blocking collectives, local(): lax.all_gather(prolong_columns, 'row', axis=0, tiled=True)  81.6 us
    all_gather x1, waiting for transfers between devices, local(): lax.all_gather(blocks, 'row', axis=0, tiled=True)  57.7 us
    reduce_scatter x1, waiting for transfers between devices, local(): lax.psum_scatter(partial_value, 'col', scatter_dimension=1, tiled=True)  42 us
    dot_general x1, matrix products, make_folder(): jnp.einsum('mn,nbc->mbc', matches.astype(jnp.bfloat16), piece_blocks, pre...  11.2 us
    reshape x1, local copies, waits for them, and re-layouts, local(): partial_value.reshape(bricks * BRICK, pattern.shape[0] * BRICK)  5.8 us
    dot_general x1, matrix products, local(): jnp.einsum('ikqs,ikaqc->iasc', matches, products, precision=lax.Precision...  5.43 us
  transfers between devices with their start and end apart: 2, of which 2 were waited for; matrix products, arithmetic and copies ran while one was open for 1% of the time, Pallas kernels for 0%

commit v1 on v0

v1 whole, which is shorter than its diff:
```python
import functools

import jax
import jax.numpy as jnp
from jax import lax
from jax.experimental import pallas as pl
from jax.experimental.pallas import tpu as pltpu
from jax.sharding import PartitionSpec as P

BRICK = 64
A_SLOTS = 24
COLS = 4
SLICE = BRICK // COLS
NEAR_SLOTS = 16
FAR_SLOTS = 16
OWN_BASE = NEAR_SLOTS + FAR_SLOTS
COLUMN_SLOTS = OWN_BASE + 4
OFFSETS = (-2, -1, 1, 2)
MESH = pl.DeviceIdType.MESH


def left_slot(step):
    return 2 * step - 1 if step else 0


def right_slot(step):
    return 2 * step


def ring_slot(distance, size):
    half = size // 2
    return jnp.where(
        distance == 0,
        0,
        jnp.where(distance <= half, 2 * distance - 1, 2 * (size - distance)),
    )


def gather_kernel(
    depth_z,
    depth_y,
    columns,
    counts,
    brick_ids,
    a_hbm,
    p_ref,
    slots,
    a_all,
    halo,
    ids_out,
    buf_a,
    buf_b,
    buf_i,
    send_sem,
    recv_sem,
    local_sem,
):
    slabs = depth_z * depth_y * 2
    fine = slabs * 4
    row = lax.axis_index("row")
    col = lax.axis_index("col")
    core = row % 2
    y = (row // 2) % depth_y
    z = row // (2 * depth_y)

    def at(zz, yy, cc):
        return {"row": (zz * depth_y + yy) * 2 + cc, "col": col}

    y_plus = at(z, (y + 1) % depth_y, core)
    y_minus = at(z, (y + depth_y - 1) % depth_y, core)
    z_plus = at((z + 1) % depth_z, y, core)
    z_minus = at((z + depth_z - 1) % depth_z, y, core)
    partner = at(z, y, 1 - core)
    halo_peers = [{"row": (row + o + slabs) % slabs, "col": col} for o in OFFSETS]
    x_peers = [{"row": row, "col": (col + o) % COLS} for o in (1, 2, 3)]

    barrier = pltpu.get_barrier_semaphore()
    peers = [y_plus, y_minus, z_plus, z_minus, partner] + halo_peers + x_peers
    for peer in peers:
        pl.semaphore_signal(barrier, inc=1, device_id=peer, device_id_type=MESH)

    rows = pl.ds(pl.multiple_of(col * SLICE, SLICE), SLICE)
    own_copies = [
        pltpu.make_async_copy(p_ref.at[0:2, rows, :], buf_a.at[0:2], local_sem.at[0]),
        pltpu.make_async_copy(p_ref.at[2:4, rows, :], buf_b.at[0:2], local_sem.at[1]),
        pltpu.make_async_copy(a_hbm, a_all.at[col], local_sem.at[2]),
    ]
    for copy in own_copies:
        copy.start()
    lane = lax.broadcasted_iota(jnp.int32, (1, 128), 1)
    id_row = jnp.zeros((1, 128), jnp.int32)
    for i in range(4):
        for q in range(2):
            id_row = jnp.where(lane == 2 * i + q, brick_ids[i, q], id_row)
    buf_i[0] = id_row
    own_copies[0].wait()
    own_copies[1].wait()
    pl.semaphore_wait(barrier, len(peers))

    started = []
    events = []
    done = set()
    table = {}

    def message(name, time, needs, src, dst, device):
        index = len(events)
        copy = pltpu.make_async_remote_copy(
            src_ref=src,
            dst_ref=dst,
            send_sem=send_sem.at[index],
            recv_sem=recv_sem.at[index],
            device_id=device,
            device_id_type=MESH,
        )
        table[name] = copy
        events.append((time, index, tuple(needs), copy))

    hop = 1.7

    def line(tag, buf, width, size, plus, minus):
        for step in range(1, size // 2 + 1):
            for way, device, slot, last in (
                ("L", plus, left_slot, size // 2),
                ("R", minus, right_slot, (size - 1) // 2),
            ):
                if step > last:
                    continue
                message(
                    (tag, "line", way, step),
                    hop * (step - 1),
                    [(tag, "line", way, step - 1)] if step > 1 else [],
                    buf.at[pl.ds(width * slot(step - 1), width)],
                    buf.at[pl.ds(width * slot(step), width)],
                    device,
                )

    def line_needs(tag, size, lo, hi):
        names, depth = [], 0
        for way, slot, last in (("L", left_slot, size // 2), ("R", right_slot, (size - 1) // 2)):
            for step in range(1, last + 1):
                if lo <= slot(step) < hi:
                    names.append((tag, "line", way, step))
                    depth = max(depth, step)
        return names, depth

    def ring(tag, buf, width, inner, size, pieces, plus, minus, pace):
        half = size // 2
        for step in range(1, half + 1):
            for way, device, slot in (("L", plus, left_slot), ("R", minus, right_slot)):
                for at_piece, (lo, hi) in enumerate(pieces):
                    target = slot(step)
                    if step == half and size % 2 == 0:
                        mine = at_piece < (len(pieces) + 1) // 2
                        if mine != (way == "L"):
                            continue
                        target = size - 1
                    names, depth = line_needs(tag, inner, lo, hi)
                    if step > 1:
                        names = [(tag, "ring", way, step - 1, at_piece)]
                    message(
                        (tag, "ring", way, step, at_piece),
                        hop * depth + pace * (step - 1),
                        names,
                        buf.at[pl.ds(width * (slot(step - 1) * inner + lo), width * (hi - lo))],
                        buf.at[pl.ds(width * (target * inner + lo), width * (hi - lo))],
                        device,
                    )

    def forward(tag, buf, width, inner, size, pieces, pace, groups):
        total = width * inner * size
        for lo, hi in groups:
            needs, when = [], 0.0
            names, depth = line_needs(tag, inner, 0, inner)
            for chunk in range(lo, hi):
                if chunk == 0:
                    needs += names
                    when = max(when, hop * depth)
                    continue
                step = (chunk + 1) // 2
                for at_piece in range(len(pieces)):
                    if chunk == size - 1 and size % 2 == 0:
                        way = "L" if at_piece < (len(pieces) + 1) // 2 else "R"
                    else:
                        way = "L" if chunk % 2 else "R"
                    needs.append((tag, "ring", way, step, at_piece))
                when = max(when, hop * depth + pace * step)
            span = width * inner
            message(
                (tag, "forward", lo),
                when + 0.1,
                needs,
                buf.at[pl.ds(span * lo, span * (hi - lo))],
                buf.at[pl.ds(total + span * lo, span * (hi - lo))],
                partner,
            )

    def pairs(size):
        groups = [(0, 1)] + [(k, min(k + 2, size)) for k in range(1, size, 2)]
        return groups

    def cut(count):
        return [(0, count // 2), (count // 2, count)]

    line("a", buf_a, 2, depth_y, y_plus, y_minus)
    line("b", buf_b, 2, depth_z, z_plus, z_minus)
    line("i", buf_i, 1, depth_y, y_plus, y_minus)
    for at_offset, (o, peer) in enumerate(zip(OFFSETS, halo_peers)):
        lands = 3 - at_offset
        message(
            ("halo", at_offset),
            0.05,
            [],
            p_ref.at[:, rows, :],
            halo.at[col, pl.ds(4 * lands, 4)],
            peer,
        )
    halo_names = [("halo", k) for k in range(4)]
    for k, peer in enumerate(x_peers):
        message(
            ("near", k), 4.0, halo_names, halo.at[col, 0:NEAR_SLOTS], halo.at[col, 0:NEAR_SLOTS], peer
        )
        message(("share", k), 0.1, [], a_hbm, a_all.at[col], peer)
    ring("a", buf_a, 2, depth_y, depth_z, cut(depth_y), z_plus, z_minus, 2.0)
    ring("b", buf_b, 2, depth_z, depth_y, cut(depth_z), y_plus, y_minus, 2.4)
    ring("i", buf_i, 1, depth_y, depth_z, [(0, depth_y)], z_plus, z_minus, 2.0)
    forward("a", buf_a, 2, depth_y, depth_z, cut(depth_y), 2.0, pairs(depth_z))
    forward("b", buf_b, 2, depth_z, depth_y, cut(depth_z), 2.4, pairs(depth_y))
    forward("i", buf_i, 1, depth_y, depth_z, [(0, depth_y)], 2.0, [(0, depth_z)])

    def await_all(names):
        for name in names:
            if name not in done:
                done.add(name)
                table[name].wait_recv()

    def decode():
        found = []
        for i in range(4):

            def body(k, carry, i=i):
                count, picks = carry[0], carry[1:]
                j = columns[i, k]
                distance = lax.rem(j - 4 * row + 8 + fine, fine)
                is_far = distance >= 20
                brick = jnp.where(
                    distance < 8,
                    distance,
                    jnp.where(distance < 12, distance - 8 + OWN_BASE, distance - 4),
                )
                place = NEAR_SLOTS + 4 * i + jnp.minimum(count, 3)
                slot = jnp.where(is_far, place, brick)
                slots[i, k] = jnp.where(k < counts[i], slot, COLUMN_SLOTS)
                picks = tuple(
                    jnp.where(is_far & (count == m), j, picks[m]) for m in range(4)
                )
                return (count + is_far.astype(jnp.int32),) + picks

            zero = jnp.int32(0)
            carry = lax.fori_loop(0, A_SLOTS, body, (zero,) * 5)
            found += list(carry[1:])
        return found

    ordered = sorted(events, key=lambda e: (e[0], e[1]))
    far = None
    for time, index, needs, copy in ordered:
        if far is None and time > 0.2:
            far = decode()
        await_all(needs)
        copy.start()
        started.append(copy)

    def place_of(slab):
        other = slab % 2
        yy = (slab // 2) % depth_y
        zz = slab // (2 * depth_y)
        apart_z = lax.rem(z - zz + depth_z, depth_z)
        apart_y = lax.rem(y - yy + depth_y, depth_y)
        side = jnp.where(other == core, 0, 1)
        slot_z = ring_slot(apart_z, depth_z)
        slot_y = ring_slot(apart_y, depth_y)
        first = (side * depth_z + slot_z) * depth_y + slot_y
        second = (side * depth_y + slot_y) * depth_z + slot_z
        return first, second

    for name in list(table):
        if name[0] in "abi":
            await_all([name])
    for f in range(FAR_SLOTS):
        slab, i = far[f] // 4, far[f] % 4
        first, second = place_of(slab)
        low = buf_a[2 * first + i % 2]
        high = buf_b[2 * second + i % 2]
        halo[col, NEAR_SLOTS + f] = jnp.where(i < 2, low, high)
        ids_out[NEAR_SLOTS + f] = jnp.where(lane // 2 == i, buf_i[first], 0)
    await_all([("near", k) for k in range(3)])
    last = []
    base = len(events)
    for k, peer in enumerate(x_peers):
        copy = pltpu.make_async_remote_copy(
            src_ref=halo.at[col, pl.ds(NEAR_SLOTS, FAR_SLOTS)],
            dst_ref=halo.at[col, pl.ds(NEAR_SLOTS, FAR_SLOTS)],
            send_sem=send_sem.at[base + k],
            recv_sem=recv_sem.at[base + k],
            device_id=peer,
            device_id_type=MESH,
        )
        copy.start()
        last.append(copy)
    for at_offset, o in enumerate(OFFSETS):
        first, _ = place_of(lax.rem(row + o + slabs, slabs))
        for i in range(4):
            ids_out[4 * at_offset + i] = jnp.where(lane // 2 == i, buf_i[first], 0)
    for i in range(4):
        ids_out[OWN_BASE + i] = jnp.where(lane // 2 == i, id_row, 0)
    await_all([("share", k) for k in range(3)])
    own_copies[2].wait()
    for copy in started:
        copy.wait_send()
    for copy in last:
        copy.wait()


def message_count(depth_z, depth_y):
    def pieces(size):
        return 2 * (2 * (size // 2 - 1)) + 2

    lines = 2 * (depth_y - 1) + (depth_z - 1)
    rings = pieces(depth_z) + pieces(depth_y) + depth_z - 1
    forwards = (depth_z // 2 + 1) + (depth_y // 2 + 1) + 1
    return lines + rings + forwards + 4 + 3 + 3 + 3


def compute_kernel(
    slots, pattern, a_all, halo, p_ref, ids, restrict, out, acc, masks, lhs, weights
):
    col = lax.axis_index("col")
    width = out.shape[1]
    share = a_all.shape[2] // BRICK
    acc[...] = jnp.zeros_like(acc)
    for i in range(4):
        r_part = restrict[:, BRICK * i : BRICK * (i + 1)]
        for x in range(COLS):
            t = lax.dot_general(
                a_all[x, BRICK * i : BRICK * (i + 1), :],
                r_part,
                (((0,), (1,)), ((), ())),
                preferred_element_type=jnp.float32,
            )
            for k in range(share):
                slot = slots[i, share * x + k]
                acc[slot] = acc[slot] + t[BRICK * k : BRICK * (k + 1), :]

    lane = lax.broadcasted_iota(jnp.int32, (1, 128), 1)
    low_half = lane < BRICK
    id_rows = ids[...]
    for q in range(2):
        kept = jnp.where((lane % 2 == q)[None], id_rows, 0)
        names = jnp.sum(kept.astype(jnp.float32), axis=2, keepdims=True).astype(jnp.int32)
        for pair in range(width // 128):
            first = pattern[0, col * (width // BRICK) + 2 * pair]
            second = pattern[0, col * (width // BRICK) + 2 * pair + 1]
            wanted = jnp.where(low_half, first, second)
            masks[q, :, :, 128 * pair : 128 * (pair + 1)] = (names == wanted[None]).astype(jnp.float32)

    def place(c, x, piece):
        wide = piece.astype(jnp.float32)
        turned = pltpu.roll(wide, BRICK, 1)
        for q in range(2):
            both = jnp.where(low_half, wide, turned) if q == 0 else jnp.where(low_half, turned, wide)
            for pair in range(width // 128):
                lanes = slice(128 * pair, 128 * (pair + 1))
                mask = masks[q, c, :, lanes]
                weights[q, c, SLICE * x : SLICE * (x + 1), lanes] = (both * mask).astype(
                    jnp.bfloat16
                )

    def spread(c, _):
        for x in range(COLS):
            place(c, x, halo[x, c])
        return 0

    lax.fori_loop(0, OWN_BASE, spread, 0)

    def spread_own(i, _):
        for x in range(COLS):
            place(OWN_BASE + i, x, p_ref[i, SLICE * x : SLICE * (x + 1), :])
        return 0

    lax.fori_loop(0, 4, spread_own, 0)

    depth = COLUMN_SLOTS * BRICK
    turned = jnp.transpose(acc[0:COLUMN_SLOTS].reshape(depth, 128))
    high = turned.astype(jnp.bfloat16)
    lhs[0:128, :] = high
    lhs[128:256, :] = (turned - high.astype(jnp.float32)).astype(jnp.bfloat16)
    total = jnp.dot(
        lhs[...], weights[0].reshape(depth, width), preferred_element_type=jnp.float32
    ) + jnp.dot(lhs[...], weights[1].reshape(depth, width), preferred_element_type=jnp.float32)
    out[...] = total[0:128] + total[128:256]


def build(mesh, depth_z, depth_y):
    vmem = pl.BlockSpec(memory_space=pltpu.VMEM)
    smem = pl.BlockSpec(memory_space=pltpu.SMEM)
    anywhere = pl.BlockSpec(memory_space=pl.ANY)

    def local(
        fine_matrix, fine_columns, fine_counts, prolong, prolong_columns, restrict_rows, coarse_pattern
    ):
        blocks = prolong.reshape(4, BRICK, 128)
        share = fine_matrix.shape[1]
        devices = depth_z * depth_y * 2
        count = message_count(depth_z, depth_y)
        slots, a_all, halo, ids = pl.pallas_call(
            functools.partial(gather_kernel, depth_z, depth_y),
            name="exchange",
            out_shape=(
                jax.ShapeDtypeStruct((4, A_SLOTS), jnp.int32),
                jax.ShapeDtypeStruct((COLS, 256, share), jnp.bfloat16),
                jax.ShapeDtypeStruct((COLS, OWN_BASE, SLICE, 128), jnp.bfloat16),
                jax.ShapeDtypeStruct((COLUMN_SLOTS, 1, 128), jnp.int32),
            ),
            in_specs=[smem, smem, smem, anywhere, vmem],
            out_specs=(smem, vmem, vmem, vmem),
            scratch_shapes=[
                pltpu.VMEM((2 * devices, SLICE, 128), jnp.bfloat16),
                pltpu.VMEM((2 * devices, SLICE, 128), jnp.bfloat16),
                pltpu.VMEM((devices, 1, 128), jnp.int32),
                pltpu.SemaphoreType.DMA((count,)),
                pltpu.SemaphoreType.DMA((count,)),
                pltpu.SemaphoreType.DMA((3,)),
            ],
            compiler_params=pltpu.CompilerParams(collective_id=0, has_side_effects=True),
        )(fine_columns, fine_counts, prolong_columns, fine_matrix, blocks)
        width = coarse_pattern.shape[1] * BRICK // COLS
        return pl.pallas_call(
            compute_kernel,
            name="assemble",
            out_shape=jax.ShapeDtypeStruct((128, width), jnp.float32),
            in_specs=[smem, smem, vmem, vmem, vmem, vmem, vmem],
            out_specs=vmem,
            scratch_shapes=[
                pltpu.VMEM((COLUMN_SLOTS + 1, BRICK, 128), jnp.float32),
                pltpu.VMEM((2, COLUMN_SLOTS, 1, width), jnp.float32),
                pltpu.VMEM((256, COLUMN_SLOTS * BRICK), jnp.bfloat16),
                pltpu.VMEM((2, COLUMN_SLOTS, BRICK, width), jnp.bfloat16),
            ],
        )(slots, coarse_pattern, a_all, halo, blocks, ids, restrict_rows)

    return jax.shard_map(
        local,
        mesh=mesh,
        in_specs=(
            P("row", "col"),
            P("row", None),
            P("row"),
            P("row", None),
            P("row", None),
            P("row", None),
            P("row", None),
        ),
        out_specs=P("row", "col"),
        check_vma=False,
    )


def solution(mesh):
    return build(mesh, 12, 8)
```

time: 226 us -> 70.7 us (0.31)
  waiting for transfers between devices: 100 us -> 0 us
  blocking collectives: 81.6 us -> 0 us
  Pallas kernels: 0 us -> 69.2 us
  matrix products: 18.9 us -> 0 us
  between operations: 13.5 us -> 0.01 us
  local copies, waits for them, and re-layouts: 10 us -> 1.34 us
    all_gather x1 -> x0, blocking collectives: 81.6 us -> none  [local(): lax.all_gather(prolong_columns, 'row', axis=0, tiled=True)]
    pallas_call x0 -> x2, Pallas kernels: none -> 69.2 us  [the longest x1 60.3 us: local(): pl.pallas_call(functools.partial(gather_kernel, depth_z, depth_y), name='...]
    all_gather x1 -> x0, waiting for transfers between devices: 57.7 us -> none  [local(): lax.all_gather(blocks, 'row', axis=0, tiled=True)]
    reduce_scatter x1 -> x0, waiting for transfers between devices: 42 us -> none  [local(): lax.psum_scatter(partial_value, 'col', scatter_dimension=1, tiled=True)]
    dot_general x4 -> x0, matrix products: 18.9 us -> none  [the longest x1 11.2 us: make_folder(): jnp.einsum('mn,nbc->mbc', matches.astype(jnp.bfloat16), piece_blocks, pre...]
    reshape x3 -> x0, local copies, waits for them, and re-layouts: 7.92 us -> none  [the longest x1 5.8 us: local(): partial_value.reshape(bricks * BRICK, pattern.shape[0] * BRICK)]
  transfers between devices with their start and end apart: 2 -> 0, of which waited for: 2 -> 0; matrix products, arithmetic and copies ran while one was open for 1% -> 0% of each run, Pallas kernels for 0% -> 0%
where the time goes in v1:
time: 70.7 us; the launch traced here: 70.5 us
  Pallas kernels  69.2 us (98%)
  local copies, waits for them, and re-layouts  1.34 us (2%)
    pallas_call x1, Pallas kernels, local(): pl.pallas_call(functools.partial(gather_kernel, depth_z, depth_y), name='...  60.3 us
    pallas_call x1, Pallas kernels, local(): pl.pallas_call(compute_kernel, name='assemble', out_shape=jax.ShapeDtypeS...  8.85 us

profile of v1, /device:TPU:1, one launch (start us, length us, event | category | flops | bytes accessed | tf_op | source)
XLA Modules:
  0.0 70.5 jit_solution(396622298732354474)
XLA Ops:
  0.0 0.0 copy-start
  0.0 0.7 copy-done
  0.7 0.7 copy.8.brick_ids
  1.3 60.3 %exchange.1 = (s32[4,24]{1,0:T(4,128)}, bf16[4,256,384]{2,1,0:T(8,128)(2,1)}, bf16[4,32,16,128]{3,2,1,0:T(8,128)(2,1)}, s32[36,1,128]{2,1,0:T(1,128)}) custom-call(s32[4,24]{1,0:T(4,128)} %columns.1, s32[4]{0:T(128)} %counts.1, s32[4,2]{1,0:T(4,128)} %copy.8.brick_ids, bf16[256,384]{1,0:T(8,128)(2,1)} %a_hbm.1, bf16[4,64,128]{2,1,0:T(8,128)(2,1)} %bitcast.1), custom_call_target="tpu_custom_call" | custom-call | tf_op jit(solution)/shard_map/exchange/pallas_call | solution.py:414
  61.7 8.8 %assemble.1 = f32[128,768]{1,0:T(8,128)} custom-call(s32[4,24]{1,0:T(4,128)} %get-tuple-element.9.slots, s32[1,48]{1,0:T(1,128)} %pattern.1, bf16[4,256,384]{2,1,0:T(8,128)(2,1)} %get-tuple-element.10.a_all, bf16[4,32,16,128]{3,2,1,0:T(8,128)(2,1)} %get-tuple-element.11.halo, bf16[4,64,128]{2,1,0:T(8,128)(2,1)} %bitcast.2, ...), custom_call_target="tpu_custom_call" | custom-call | tf_op jit(solution)/shard_map/assemble/pallas_call | solution.py:436
Async XLA Ops:
  0.0 0.7 copy-start
